TPU v7x, 32 devices: a whole 2x2x4 slice. The times are simulated.
32 devices in a mesh: dp: 8 (over z, core), ctx: 4 (over y, x).
Axes of the slice: x: 2, y: 2, z: 4, core: 2. Of those that a mesh axis runs over, the one named last changes fastest.
Arguments:
- loader_rows: bfloat16 [8192, 512], P(('dp', 'ctx')), may hold values from -60 to 60
- send_slot: int32 [8192], P(('dp', 'ctx')), may hold values from 0 to 383, as said below
- arrive_slot: int32 [8192], P(('dp', 'ctx')), may hold values from 0 to 383, as said below
- user_lengths: int32 [8, 4], P('dp'), may hold values from 1 to 768, 1024 in all within a row
- proj_weight: bfloat16 [512, 2048], replicated, may hold values from -0.25 to 0.25
- out_weight: bfloat16 [512, 512], replicated, may hold values from -0.25 to 0.25
- cotangent: bfloat16 [8192, 512], P(('dp', 'ctx')), may hold values from -6 to 6
Outputs:
- layer_out: bfloat16 [8192, 512], P(('dp', 'ctx'))
- row_grads: bfloat16 [8192, 512], P(('dp', 'ctx'))
- proj_grad: float32 [512, 2048], replicated
- out_grad: float32 [512, 512], replicated
Inputs may be any that keep to these rules, and one draw needn't show every extreme that they name: `send_slot`: on each loader device its 256 entries are distinct slots d * 12 + k, d the owner device and k counting that owner's rows from this loader from 0; no loader sends more than 12 rows to one owner and some pairs send exactly 12; the number of rows from loader s to owner d depends only on (d - s) mod (8 * 4). `arrive_slot`: on each owner device its 256 entries are distinct slots s * 12 + k, the k-th row that loader s sends to it; every owner receives exactly 256 rows.
All inputs are finite; a program needn't handle non-finite values.
Results may differ from a plain program's by a relative error of at most 0.009.
Values may be sent and summed in bfloat16 or wider, within the bound.
No kernel may reach another device: no remote copies, remote signals or barrier semaphores. Data moves between devices by JAX's collectives and lax.ppermute only.
A program may use at most 128 MiB of HBM per device.

v0:
```python
import jax
import jax.numpy as jnp
from jax import lax
from jax.sharding import PartitionSpec as P

HEADS = 8
norm_eps = 1e-05


def normalize(values):
    centre = values - jnp.mean(values, axis=-1, keepdims=True)
    inverse = lax.rsqrt(jnp.mean(centre * centre, axis=-1, keepdims=True) + norm_eps)
    return (centre * inverse, inverse)


def normalize_back(grad_in, normed, inverse):
    mean_grad = jnp.mean(grad_in, axis=-1, keepdims=True)
    mean_cross = jnp.mean(grad_in * normed, axis=-1, keepdims=True)
    return (grad_in - mean_grad - normed * mean_cross) * inverse


def silu_grad(values):
    sigma = jax.nn.sigmoid(values)
    return sigma * (1.0 + values * (1.0 - sigma))


def in_blocks(step_fn, block_rows, running, pieces):
    total_rows = pieces[0].shape[0]

    def one_block(index, carry):
        start = index * block_rows
        sliced = tuple((lax.dynamic_slice_in_dim(each, start, block_rows, 0) for each in pieces))
        return step_fn(carry, sliced, start)

    return lax.fori_loop(0, total_rows // block_rows, one_block, running)


def local(loader_rows, send_slot, arrive_slot, user_lengths, proj_weight, out_weight, cotangent):
    row_count = send_slot.shape[0]
    model_width = out_weight.shape[0]
    head_dim = model_width // HEADS
    score_scale = head_dim ** (-0.5)
    group_size = lax.axis_size("ctx")
    group_count = lax.axis_size("dp")
    device_count = group_size * group_count
    per_pair = row_count // device_count
    capacity = per_pair + max(1, per_pair // 2)
    half_rows = row_count // 2
    group_total = group_size * row_count
    outgoing = (
        jnp.zeros((device_count * capacity, model_width), jnp.bfloat16)
        .at[send_slot]
        .set(loader_rows)
    )
    arrived = lax.all_to_all(
        outgoing.reshape(device_count, capacity, model_width),
        ("dp", "ctx"),
        split_axis=0,
        concat_axis=0,
        tiled=True,
    )
    own_rows = arrived.reshape(device_count * capacity, model_width)[arrive_slot]
    ends = jnp.cumsum(user_lengths[0])

    def position_of(row_index):
        device_of = row_index // row_count
        local_of = row_index % row_count
        return jnp.where(
            local_of < half_rows,
            device_of * half_rows + local_of,
            group_total - (device_of + 1) * half_rows + (local_of - half_rows),
        )

    own_pos = position_of(
        lax.axis_index("ctx") * row_count + jnp.arange(row_count, dtype=jnp.int32)
    )

    def user_of(positions):
        return jnp.sum((ends[None, :] <= positions[:, None]).astype(jnp.int32), axis=1)

    own_users = user_of(own_pos)

    def allowed_of(query_pos, query_users, key_pos, key_users):
        return (key_pos[None, :] <= query_pos[:, None]) & (
            query_users[:, None] == key_users[None, :]
        )

    def split_heads(values):
        return values.reshape(values.shape[0], HEADS, head_dim)

    def merge_heads(values):
        return values.reshape(values.shape[0], model_width)

    def piece_scores(query_part, key_part):
        return (
            jnp.einsum(
                "qhd,khd->hqk",
                split_heads(query_part),
                split_heads(key_part),
                preferred_element_type=jnp.float32,
            )
            * score_scale
        )

    rows_f = own_rows.astype(jnp.float32)
    normed, inverse_in = normalize(rows_f)
    normed_bf = normed.astype(jnp.bfloat16)
    pre = jnp.dot(normed_bf, proj_weight, preferred_element_type=jnp.float32)
    proj = (pre * jax.nn.sigmoid(pre)).astype(jnp.bfloat16)
    update_rows = proj[:, :model_width]
    value_rows = proj[:, model_width : 2 * model_width]
    query_rows = proj[:, 2 * model_width : 3 * model_width]
    key_rows = proj[:, 3 * model_width :]

    def attend_block(running, pieces, first_row):
        key_part, value_part = pieces
        key_pos = position_of(first_row + jnp.arange(key_part.shape[0], dtype=jnp.int32))
        allowed = allowed_of(own_pos, own_users, key_pos, user_of(key_pos))[None]
        scores = piece_scores(query_rows, key_part)
        weights = jnp.where(allowed, scores * jax.nn.sigmoid(scores), 0.0).astype(jnp.bfloat16)
        product = jnp.einsum(
            "hqk,khd->qhd", weights, split_heads(value_part), preferred_element_type=jnp.float32
        )
        return running + merge_heads(product)

    zeros_rows = jnp.zeros((row_count, model_width), jnp.float32)
    attended = in_blocks(
        attend_block,
        row_count,
        zeros_rows,
        (
            lax.all_gather(key_rows, "ctx", axis=0, tiled=True),
            lax.all_gather(value_rows, "ctx", axis=0, tiled=True),
        ),
    )
    att_normed, inverse_att = normalize(attended)
    update_f = update_rows.astype(jnp.float32)
    gated = (att_normed * update_f).astype(jnp.bfloat16)
    layer_rows = (rows_f + jnp.dot(gated, out_weight, preferred_element_type=jnp.float32)).astype(
        jnp.bfloat16
    )
    out_term = jnp.dot(gated.T, cotangent, preferred_element_type=jnp.float32)
    grad_gated = jnp.dot(cotangent, out_weight.T, preferred_element_type=jnp.float32)
    grad_update = grad_gated * att_normed
    grad_att = normalize_back(grad_gated * update_f, att_normed, inverse_att).astype(jnp.bfloat16)

    def query_block(running, pieces, first_row):
        key_part, value_part = pieces
        key_pos = position_of(first_row + jnp.arange(key_part.shape[0], dtype=jnp.int32))
        allowed = allowed_of(own_pos, own_users, key_pos, user_of(key_pos))[None]
        scores = piece_scores(query_rows, key_part)
        grad_weights = jnp.einsum(
            "qhd,khd->hqk",
            split_heads(grad_att),
            split_heads(value_part),
            preferred_element_type=jnp.float32,
        )
        grad_scores = jnp.where(
            allowed, grad_weights * silu_grad(scores) * score_scale, 0.0
        ).astype(jnp.bfloat16)
        product = jnp.einsum(
            "hqk,khd->qhd", grad_scores, split_heads(key_part), preferred_element_type=jnp.float32
        )
        return running + merge_heads(product)

    def key_block(running, pieces, first_row):
        query_part, grad_part = pieces
        query_pos = position_of(first_row + jnp.arange(query_part.shape[0], dtype=jnp.int32))
        allowed = allowed_of(query_pos, user_of(query_pos), own_pos, own_users)[None]
        scores = piece_scores(query_part, key_rows)
        weights = jnp.where(allowed, scores * jax.nn.sigmoid(scores), 0.0).astype(jnp.bfloat16)
        grad_weights = jnp.einsum(
            "qhd,khd->hqk",
            split_heads(grad_part),
            split_heads(value_rows),
            preferred_element_type=jnp.float32,
        )
        grad_scores = jnp.where(
            allowed, grad_weights * silu_grad(scores) * score_scale, 0.0
        ).astype(jnp.bfloat16)
        grad_key = jnp.einsum(
            "hqk,qhd->khd", grad_scores, split_heads(query_part), preferred_element_type=jnp.float32
        )
        grad_value = jnp.einsum(
            "hqk,qhd->khd", weights, split_heads(grad_part), preferred_element_type=jnp.float32
        )
        return (running[0] + merge_heads(grad_key), running[1] + merge_heads(grad_value))

    grad_query = in_blocks(
        query_block,
        row_count,
        zeros_rows,
        (
            lax.all_gather(key_rows, "ctx", axis=0, tiled=True),
            lax.all_gather(value_rows, "ctx", axis=0, tiled=True),
        ),
    )
    grad_key, grad_value = in_blocks(
        key_block,
        row_count,
        (zeros_rows, zeros_rows),
        (
            lax.all_gather(query_rows, "ctx", axis=0, tiled=True),
            lax.all_gather(grad_att, "ctx", axis=0, tiled=True),
        ),
    )
    grad_proj = jnp.concatenate([grad_update, grad_value, grad_query, grad_key], axis=1)
    grad_pre = (grad_proj * silu_grad(pre)).astype(jnp.bfloat16)
    proj_term = jnp.dot(normed_bf.T, grad_pre, preferred_element_type=jnp.float32)
    grad_normed = jnp.dot(grad_pre, proj_weight.T, preferred_element_type=jnp.float32)
    row_grads = (
        cotangent.astype(jnp.float32) + normalize_back(grad_normed, normed, inverse_in)
    ).astype(jnp.bfloat16)
    proj_sum, out_sum = lax.psum((proj_term, out_term), ("dp", "ctx"))
    grad_scale = (row_count * device_count) ** (-0.5)
    return (layer_rows, row_grads, proj_sum * grad_scale, out_sum * grad_scale)


def solution(mesh):
    placed = (
        P(("dp", "ctx"), None),
        P(("dp", "ctx")),
        P(("dp", "ctx")),
        P("dp", None),
        P(),
        P(),
        P(("dp", "ctx"), None),
    )
    return jax.shard_map(
        local,
        mesh=mesh,
        in_specs=placed,
        out_specs=(P(("dp", "ctx"), None), P(("dp", "ctx"), None), P(), P()),
        check_vma=False,
    )
```

profile of v0, /device:TPU:0, one launch (start us, length us, event | category | flops | bytes accessed | tf_op | source)
XLA Modules:
  0.0 400.7 jit_solution(9366824799308477023)
XLA Ops:
  8.0 2.0 scatter_custom_fusion
  10.9 7.3 %all-to-all-start = ((bf16[32,12,512]{2,1,0:T(8,128)(2,1)}), bf16[32,12,512]{2,1,0:T(8,128)(2,1)S(1)}, u32[]{:S(2)}, u32[]{:S(2)}) async-start(bf16[32,12,512]{2,1,0:T(8,128)(2,1)} %reshape.616), calls=%async_computation | async-start | bytes 1048576 | tf_op jit(solution)/shard_map/all_to_all | solution.py:55
  18.4 16.2 %all-to-all-done = bf16[32,12,512]{2,1,0:T(8,128)(2,1)S(1)} async-done(((bf16[32,12,512]{2,1,0:T(8,128)(2,1)}), bf16[32,12,512]{2,1,0:T(8,128)(2,1)S(1)}, u32[]{:S(2)}, u32[]{:S(2)}) %all-to-all-start) | async-done | bytes 393248 | tf_op jit(solution)/shard_map/all_to_all | solution.py:55
  36.2 2.1 multiply_convert_fusion
  45.8 18.7 %all-gather.5.cloned.1.call-done = bf16[1024,512]{1,0:T(8,128)(2,1)} async-done(((bf16[256,512]{1,0:T(8,128)(2,1)}), bf16[1024,512]{1,0:T(8,128)(2,1)}) %all-gather.5.cloned.1.call-update) | async-done | bytes 1048592 | tf_op jit(solution)/shard_map/all_gather | solution.py:133
  64.5 2.3 copy.48
  66.8 26.7 %all-gather.7.cloned.1.call-done = bf16[1024,512]{1,0:T(8,128)(2,1)} async-done(((bf16[256,512]{1,0:T(8,128)(2,1)}), bf16[1024,512]{1,0:T(8,128)(2,1)}) %all-gather.7.cloned.1.call-update) | async-done | bytes 1048592 | tf_op jit(solution)/shard_map/all_gather | solution.py:132
  93.5 2.3 copy.49
  95.7 17.4 %while.50 = (s32[]{:T(128)}, f32[256,512]{0,1:T(8,128)S(1)}, bf16[1024,512]{0,1:T(8,128)(2,1)}, s32[256]{0:T(256)S(1)}, s32[4]{0:T(128)S(1)}, /*index=5*/bf16[10...) while((s32[]{:T(128)}, f32[256,512]{0,1:T(8,128)S(1)}, ...), condition=%wide.region_7.8_spmd.clone, body=%wide.region_5.7_spmd.clone.sunk | while | flops 138364160 | bytes 4071625 | solution.py:35
  97.9 2.1 fusion.118
  102.2 2.1 fusion.118
  106.6 2.1 fusion.118
  111.0 2.1 fusion.118
  115.4 2.1 multiply_convert_fusion.1
  118.6 46.4 %while.52 = (s32[]{:T(128)}, f32[256,512]{0,1:T(8,128)}, bf16[1024,512]{0,1:T(8,128)(2,1)}, s32[256]{0:T(256)S(1)}, s32[4]{0:T(128)S(1)}, /*index=5*/bf16[1024,5...) while((s32[]{:T(128)}, f32[256,512]{0,1:T(8,128)}, ...), condition=%wide.region_17.18_spmd.clone, body=%wide.region_15.17_spmd.clone.sunk | while | flops 208094464 | bytes 12984529 | solution.py:35
  119.9 3.2 fusion.133
  123.2 2.9 copy.73
  126.0 2.3 fusion.134
  130.7 3.2 fusion.133
  133.9 2.9 copy.73
  136.8 2.3 fusion.134
  142.7 3.2 fusion.133
  145.9 2.9 copy.73
  148.8 2.3 fusion.134
  154.5 3.2 fusion.133
  157.7 2.9 copy.73
  160.6 2.3 fusion.134
  164.9 2.1 copy.61
  167.0 2.3 fusion.70
  169.4 61.8 %while.51 = (s32[]{:T(128)}, f32[256,512]{0,1:T(8,128)S(1)}, f32[256,512]{0,1:T(8,128)}, bf16[1024,512]{1,0:T(8,128)(2,1)}, s32[4]{0:T(128)S(1)}, /*index=5*/s32...) while((s32[]{:T(128)}, f32[256,512]{0,1:T(8,128)S(1)}, ...), condition=%wide.region_14.15_spmd.clone, body=%wide.region_12.14_spmd.clone.sunk | while | flops 279135488 | bytes 18555156 | solution.py:35
  170.5 2.8 fusion.125
  175.4 3.8 fusion.127
  179.2 3.3 fusion.126
  185.9 2.8 fusion.125
  190.8 3.8 fusion.127
  194.6 3.3 fusion.126
  201.4 2.8 fusion.125
  206.2 3.8 fusion.127
  210.0 3.3 fusion.126
  216.8 2.8 fusion.125
  221.7 3.8 fusion.127
  225.5 3.3 fusion.126
  231.1 2.1 copy.60
  234.2 3.0 fusion.45
  237.2 2.9 fusion.63
  240.1 2.1 fusion.46
  244.1 144.0 %all-reduce.3.cloned.1.call-done = (f32[512,2048]{1,0:T(8,128)}, f32[512,512]{1,0:T(8,128)}) async-done(((f32[512,2048]{1,0:T(8,128)}, f32[512,512]{1,0:T(8,128)}), (f32[512,2048]{1,0:T(8,128)}, f32[512,512]{1,0:T(8,128)})) %all-reduce.3.cloned.1.call-update) | async-done | bytes 5242896 | tf_op jit(solution)/shard_map/psum | solution.py:214
  388.1 5.0 %broadcast_multiply_fusion = f32[512,2048]{1,0:T(8,128)} fusion(f32[512,2048]{1,0:T(8,128)} %get-tuple-element.919), kind=kLoop, calls=%fused_computation.106 | loop fusion | flops 1048576 | bytes 8388608 | tf_op jit(solution)/shard_map/mul | solution.py:216
  (157 shorter events, 61.4 us)
Async XLA Ops:
  7.2 29.0 %copy-start = (bf16[512,2048]{1,0:T(8,128)(2,1)S(1)}, bf16[512,2048]{1,0:T(8,128)(2,1)}, u32[]{:S(2)}) copy-start(bf16[512,2048]{1,0:T(8,128)(2,1)} %param.17) | copy-start | bytes 6291460
  7.2 11.1 %copy-start.9 = (s32[256]{0:T(256)S(1)}, s32[256]{0:T(256)}, u32[]{:S(2)}) copy-start(s32[256]{0:T(256)} %param.15) | copy-start | bytes 3076
  10.9 23.6 %all-to-all-start = ((bf16[32,12,512]{2,1,0:T(8,128)(2,1)}), bf16[32,12,512]{2,1,0:T(8,128)(2,1)S(1)}, u32[]{:S(2)}, u32[]{:S(2)}) async-start(bf16[32,12,512]{2,1,0:T(8,128)(2,1)} %reshape.616), calls=%async_computation | async-start | bytes 1048576 | tf_op jit(solution)/shard_map/all_to_all | solution.py:55
  18.3 46.2 %all-gather.5.cloned.1.call-start = ((), (), s32[]{:S(2)}) async-start(), calls=%async_computation.1 | async-start | bytes 1310720 | tf_op jit(solution)/shard_map/all_gather | solution.py:133
  38.3 1.0 copy-start.7
  38.3 2.7 copy-start.10
  40.1 5.6 %copy-start.5 = (bf16[256,512]{1,0:T(8,128)(2,1)}, bf16[256,512]{1,0:T(8,128)(2,1)S(1)}, u32[]{:S(2)}) copy-start(bf16[256,512]{1,0:T(8,128)(2,1)S(1)} %get-tuple-element.934) | copy-start | bytes 786436
  40.2 53.3 %all-gather.7.cloned.1.call-start = ((), (), s32[]{:S(2)}) async-start(), calls=%async_computation.2 | async-start | bytes 1310720 | tf_op jit(solution)/shard_map/all_gather | solution.py:132
  40.9 128.5 %all-gather.9.cloned.1.call-start = ((), (), s32[]{:S(2)}) async-start(), calls=%async_computation.3 | async-start | bytes 1310720 | tf_op jit(solution)/shard_map/all_gather | solution.py:203
  45.8 123.6 %all-gather.11.cloned.1.call-start = ((), (), s32[]{:S(2)}) async-start(), calls=%async_computation.4 | async-start | bytes 1310720 | tf_op jit(solution)/shard_map/all_gather | solution.py:204
  117.5 0.8 copy-start.4
  118.3 269.8 %all-reduce.3.cloned.1.call-start = ((), (), s32[]{:S(2)}) async-start(), calls=%async_computation.5 | async-start | bytes 10485760 | tf_op jit(solution)/shard_map/psum | solution.py:214
  164.9 4.4 %copy-start.1 = (f32[256,512]{0,1:T(8,128)S(1)}, f32[256,512]{0,1:T(8,128)}, u32[]{:S(2)}) copy-start(f32[256,512]{0,1:T(8,128)} %custom-call.1) | copy-start | bytes 1572868
  179.2 3.3 copy-start.2
  184.0 0.8 copy-start.3
  194.6 3.3 copy-start.2
  199.4 0.8 copy-start.3
  210.0 3.3 copy-start.2
  214.9 0.8 copy-start.3
  225.5 3.3 copy-start.2
  230.3 0.8 copy-start.3
  242.2 0.9 copy-start.6
  388.1 5.0 %copy-start.8 = (f32[512,512]{1,0:T(8,128)S(1)}, f32[512,512]{1,0:T(8,128)}, u32[]{:S(2)}) copy-start(f32[512,512]{1,0:T(8,128)} %get-tuple-element.920) | copy-start | bytes 3145732
Sparse Core Ops, SparseCore 0:
  40.3 24.1 all-gather.4
  66.9 26.4 all-gather.6
  95.3 26.5 all-gather.8
  123.6 26.4 all-gather.10
  240.2 147.8 all-reduce.2
where the time goes:
time: 403 us; the launch traced here: 401 us
  waiting for transfers between devices  206 us (51%)
  matrix products  82.1 us (20%)
  local copies, waits for them, and re-layouts  59.7 us (15%)
  other arithmetic  30.5 us (8%)
  between operations  14 us (3%)
  starting transfers between devices  7.71 us (2%)
    psum x1, waiting for transfers between devices, local(): proj_sum, out_sum = lax.psum((proj_term, out_term), ('dp', 'ctx'))  144 us
    all_gather x1, waiting for transfers between devices, local(): lax.all_gather(key_rows, 'ctx', axis=0, tiled=True)  26.7 us
    dot_general x8, matrix products, piece_scores(): jnp.einsum('qhd,khd->hqk', split_heads(query_part), split_heads(key_part)...  24.1 us
    dynamic_slice x24, local copies, waits for them, and re-layouts, one_block(): lax.dynamic_slice_in_dim(each, start, block_rows, 0)  23.5 us
    all_gather x1, waiting for transfers between devices, local(): lax.all_gather(value_rows, 'ctx', axis=0, tiled=True)  18.7 us
    all_to_all x1, waiting for transfers between devices, local(): lax.all_to_all(outgoing.reshape(device_count, capacity, model_width), ('d...  16.2 us
    dot_general x4, matrix products, key_block(): jnp.einsum('hqk,qhd->khd', grad_scores, split_heads(query_part), preferre...  15.2 us
    dot_general x4, matrix products, key_block(): jnp.einsum('hqk,qhd->khd', weights, split_heads(grad_part), preferred_ele...  13.1 us
  transfers between devices with their start and end apart: 6, of which 4 were waited for; matrix products, arithmetic and copies ran while one was open for 22% of the time, Pallas kernels for 0%

commit v1 on v0

--- a/solution.py
+++ b/solution.py
@@ -5,6 +5,18 @@
 
 HEADS = 8
 norm_eps = 1e-05
+
+
+def gather_by_bits(x, axis, dim):
+    ways, here = (lax.axis_size(axis), lax.axis_index(axis))
+    grown, reach = (x, 1)
+    while reach < ways:
+        theirs = lax.ppermute(grown, axis, [(d, d ^ reach) for d in range(ways)])
+        mine_first = jnp.concatenate([grown, theirs], axis=dim)
+        theirs_first = jnp.concatenate([theirs, grown], axis=dim)
+        grown = jnp.where(here & reach == 0, mine_first, theirs_first)
+        reach = 2 * reach
+    return grown
 
 
 def normalize(values):
@@ -128,10 +140,7 @@
         attend_block,
         row_count,
         zeros_rows,
-        (
-            lax.all_gather(key_rows, "ctx", axis=0, tiled=True),
-            lax.all_gather(value_rows, "ctx", axis=0, tiled=True),
-        ),
+        (gather_by_bits(key_rows, "ctx", 0), lax.all_gather(value_rows, "ctx", axis=0, tiled=True)),
     )
     att_normed, inverse_att = normalize(attended)
     update_f = update_rows.astype(jnp.float32)

time: 403 us -> 391 us (0.970)
  waiting for transfers between devices: 206 us -> 180 us
  local copies, waits for them, and re-layouts: 59.7 us -> 66.8 us
  other arithmetic: 30.5 us -> 35.4 us
    all_gather x1, waiting for transfers between devices: 26.7 us -> 0.02 us  [local(): lax.all_gather(key_rows, 'ctx', axis=0, tiled=True)]
    ppermute x0 -> x2, waiting for transfers between devices: none -> 21.2 us  [gather_by_bits(): theirs = lax.ppermute(grown, axis, [(d, d ^ reach) for d in range(ways)])]
    all_gather x1, waiting for transfers between devices: 18.7 us -> 0.01 us  [local(): lax.all_gather(value_rows, 'ctx', axis=0, tiled=True)]
    dynamic_slice x24 -> x40, local copies, waits for them, and re-layouts: 23.5 us -> 34 us  [one_block(): lax.dynamic_slice_in_dim(each, start, block_rows, 0)]
    select_n x0 -> x2, other arithmetic: none -> 4.89 us  [gather_by_bits(): grown = jnp.where(here & reach == 0, mine_first, theirs_first)]
    unnamed x24 -> x25, local copies, waits for them, and re-layouts: 10.9 us -> 7.71 us
  transfers between devices with their start and end apart: 6 -> 8, of which waited for: 4 -> 4; matrix products, arithmetic and copies ran while one was open for 22% -> 25% of each run, Pallas kernels for 0% -> 0%
where the time goes in v1:
time: 391 us; the launch traced here: 388 us
  waiting for transfers between devices  180 us (46%)
  matrix products  82 us (21%)
  local copies, waits for them, and re-layouts  66.8 us (17%)
  other arithmetic  35.4 us (9%)
  between operations  14 us (4%)
  starting transfers between devices  9.75 us (2%)
    psum x1, waiting for transfers between devices, local(): proj_sum, out_sum = lax.psum((proj_term, out_term), ('dp', 'ctx'))  142 us
    dynamic_slice x40, local copies, waits for them, and re-layouts, one_block(): lax.dynamic_slice_in_dim(each, start, block_rows, 0)  34 us
    dot_general x8, matrix products, piece_scores(): jnp.einsum('qhd,khd->hqk', split_heads(query_part), split_heads(key_part)...  24.1 us
    ppermute x2, waiting for transfers between devices, gather_by_bits(): theirs = lax.ppermute(grown, axis, [(d, d ^ reach) for d in range(ways)])  21.2 us
    all_to_all x1, waiting for transfers between devices, local(): lax.all_to_all(outgoing.reshape(device_count, capacity, model_width), ('d...  16.2 us
    dot_general x4, matrix products, key_block(): jnp.einsum('hqk,qhd->khd', grad_scores, split_heads(query_part), preferre...  15.2 us
    dot_general x4, matrix products, key_block(): jnp.einsum('hqk,qhd->khd', weights, split_heads(grad_part), preferred_ele...  13.1 us
    mul x4, local copies, waits for them, and re-layouts, silu_grad(): return sigma * (1.0 + values * (1.0 - sigma))  11.6 us
  transfers between devices with their start and end apart: 8, of which 4 were waited for; matrix products, arithmetic and copies ran while one was open for 25% of the time, Pallas kernels for 0%

profile of v1, /device:TPU:0, one launch (start us, length us, event | category | flops | bytes accessed | tf_op | source)
XLA Modules:
  0.0 388.4 jit_solution(6710774304577252571)
XLA Ops:
  8.0 2.0 scatter_custom_fusion
  10.9 7.3 %all-to-all-start = ((bf16[32,12,512]{2,1,0:T(8,128)(2,1)}), bf16[32,12,512]{2,1,0:T(8,128)(2,1)S(1)}, u32[]{:S(2)}, u32[]{:S(2)}) async-start(bf16[32,12,512]{2,1,0:T(8,128)(2,1)} %reshape.616), calls=%async_computation | async-start | bytes 1048576 | tf_op jit(solution)/shard_map/all_to_all | solution.py:67
  18.4 16.2 %all-to-all-done = bf16[32,12,512]{2,1,0:T(8,128)(2,1)S(1)} async-done(((bf16[32,12,512]{2,1,0:T(8,128)(2,1)}), bf16[32,12,512]{2,1,0:T(8,128)(2,1)S(1)}, u32[]{:S(2)}, u32[]{:S(2)}) %all-to-all-start) | async-done | bytes 393248 | tf_op jit(solution)/shard_map/all_to_all | solution.py:67
  36.2 2.1 multiply_convert_fusion
  41.2 8.1 %collective-permute-done = bf16[256,512]{1,0:T(8,128)(2,1)S(1)} collective-permute-done((bf16[256,512]{1,0:T(8,128)(2,1)}, bf16[256,512]{1,0:T(8,128)(2,1)S(1)}, u32[]{:S(2)}, u32[]{:S(2)}) %collective-permute-start) | collective-permute-done | bytes 262176 | tf_op jit(solution)/shard_map/ppermute | solution.py:14
  56.9 13.0 %collective-permute-done.1 = bf16[512,512]{1,0:T(8,128)(2,1)} collective-permute-done((bf16[512,512]{1,0:T(8,128)(2,1)}, bf16[512,512]{1,0:T(8,128)(2,1)}, u32[]{:S(2)}, u32[]{:S(2)}) %collective-permute-start.1) | collective-permute-done | bytes 524320 | tf_op jit(solution)/shard_map/ppermute | solution.py:14
  70.0 2.9 maximum_select_fusion
  72.9 2.3 copy.48
  75.2 24.0 %while.50 = (s32[]{:T(128)}, f32[256,512]{0,1:T(8,128)S(1)}, bf16[1024,512]{0,1:T(8,128)(2,1)}, s32[256]{0:T(256)S(1)}, s32[4]{0:T(128)S(1)}, /*index=5*/bf16[10...) while((s32[]{:T(128)}, f32[256,512]{0,1:T(8,128)S(1)}, ...), condition=%wide.region_7.8_spmd.clone, body=%wide.region_5.7_spmd.clone.sunk | while | flops 138364160 | bytes 4595917 | solution.py:47
  79.0 2.1 fusion.118
  84.9 2.1 fusion.118
  90.9 2.1 fusion.118
  97.0 2.1 fusion.118
  101.4 2.2 multiply_convert_fusion.1
  104.6 50.2 %while.52 = (s32[]{:T(128)}, f32[256,512]{0,1:T(8,128)}, bf16[1024,512]{1,0:T(8,128)(2,1)}, s32[256]{0:T(256)S(1)}, s32[4]{0:T(128)S(1)}, /*index=5*/bf16[1024,5...) while((s32[]{:T(128)}, f32[256,512]{0,1:T(8,128)}, ...), condition=%wide.region_17.18_spmd.clone, body=%wide.region_15.17_spmd.clone.sunk | while | flops 208094464 | bytes 13508821 | solution.py:47
  106.0 3.3 fusion.133
  109.3 2.9 copy.79
  113.2 2.3 fusion.134
  117.8 3.2 fusion.133
  121.1 2.9 copy.79
  124.9 2.3 fusion.134
  130.6 3.2 fusion.133
  133.8 2.9 copy.79
  137.8 2.3 fusion.134
  143.5 3.2 fusion.133
  146.7 2.9 copy.79
  150.5 2.4 fusion.134
  154.9 2.1 copy.61
  157.0 2.3 fusion.70
  159.3 61.7 %while.51 = (s32[]{:T(128)}, f32[256,512]{0,1:T(8,128)S(1)}, f32[256,512]{0,1:T(8,128)}, bf16[1024,512]{1,0:T(8,128)(2,1)}, s32[4]{0:T(128)S(1)}, /*index=5*/s32...) while((s32[]{:T(128)}, f32[256,512]{0,1:T(8,128)S(1)}, ...), condition=%wide.region_14.15_spmd.clone, body=%wide.region_12.14_spmd.clone.sunk | while | flops 279135488 | bytes 18555156 | solution.py:47
  160.4 2.8 fusion.125
  165.3 3.8 fusion.127
  169.1 3.3 fusion.126
  175.9 2.8 fusion.125
  180.7 3.8 fusion.127
  184.5 3.3 fusion.126
  191.3 2.8 fusion.125
  196.1 3.8 fusion.127
  199.9 3.3 fusion.126
  206.7 2.8 fusion.125
  211.5 3.8 fusion.127
  215.4 3.3 fusion.126
  221.0 2.0 copy.60
  224.0 3.0 fusion.45
  227.0 2.9 fusion.63
  229.9 2.1 fusion.46
  234.0 141.8 %all-reduce.3.cloned.1.call-done = (f32[512,2048]{1,0:T(8,128)}, f32[512,512]{1,0:T(8,128)}) async-done(((f32[512,2048]{1,0:T(8,128)}, f32[512,512]{1,0:T(8,128)}), (f32[512,2048]{1,0:T(8,128)}, f32[512,512]{1,0:T(8,128)})) %all-reduce.3.cloned.1.call-update) | async-done | bytes 5242896 | tf_op jit(solution)/shard_map/psum | solution.py:223
  375.7 5.0 %broadcast_multiply_fusion = f32[512,2048]{1,0:T(8,128)} fusion(f32[512,2048]{1,0:T(8,128)} %get-tuple-element.919), kind=kLoop, calls=%fused_computation.106 | loop fusion | flops 1048576 | bytes 8388608 | tf_op jit(solution)/shard_map/mul | solution.py:225
  (180 shorter events, 74.8 us)
Async XLA Ops:
  7.2 29.0 %copy-start = (bf16[512,2048]{1,0:T(8,128)(2,1)S(1)}, bf16[512,2048]{1,0:T(8,128)(2,1)}, u32[]{:S(2)}) copy-start(bf16[512,2048]{1,0:T(8,128)(2,1)} %param.17) | copy-start | bytes 6291460
  7.2 11.1 %copy-start.10 = (s32[256]{0:T(256)S(1)}, s32[256]{0:T(256)}, u32[]{:S(2)}) copy-start(s32[256]{0:T(256)} %param.15) | copy-start | bytes 3076
  10.9 23.6 %all-to-all-start = ((bf16[32,12,512]{2,1,0:T(8,128)(2,1)}), bf16[32,12,512]{2,1,0:T(8,128)(2,1)S(1)}, u32[]{:S(2)}, u32[]{:S(2)}) async-start(bf16[32,12,512]{2,1,0:T(8,128)(2,1)} %reshape.616), calls=%async_computation | async-start | bytes 1048576 | tf_op jit(solution)/shard_map/all_to_all | solution.py:67
  18.3 54.6 %all-gather.5.cloned.1.call-start = ((), (), s32[]{:S(2)}) async-start(), calls=%async_computation.1 | async-start | bytes 1310720 | tf_op jit(solution)/shard_map/all_gather | solution.py:143
  38.3 1.0 copy-start.8
  38.3 14.8 %copy-start.11 = (s32[1,4]{1,0:T(1,128)S(1)}, s32[1,4]{1,0:T(1,128)}, u32[]{:S(2)}) copy-start(s32[1,4]{1,0:T(1,128)} %param.16) | copy-start | bytes 52
  40.1 16.7 %copy-start.5 = (bf16[256,512]{1,0:T(8,128)(2,1)}, bf16[256,512]{1,0:T(8,128)(2,1)S(1)}, u32[]{:S(2)}) copy-start(bf16[256,512]{1,0:T(8,128)(2,1)S(1)} %get-tuple-element.930) | copy-start | bytes 786436
  40.1 15.0 %copy-start.6 = (bf16[256,512]{1,0:T(8,128)(2,1)S(1)}, bf16[256,512]{1,0:T(8,128)(2,1)}, u32[]{:S(2)}) copy-start(bf16[256,512]{1,0:T(8,128)(2,1)} %get-tuple-element.932) | copy-start | bytes 786436
  40.1 64.5 %all-gather.11.cloned.1.call-start = ((), (), s32[]{:S(2)}) async-start(), calls=%async_computation.4 | async-start | bytes 1310720 | tf_op jit(solution)/shard_map/all_gather | solution.py:203
  40.9 118.4 %all-gather.7.cloned.1.call-start = ((), (), s32[]{:S(2)}) async-start(), calls=%async_computation.2 | async-start | bytes 1310720 | tf_op jit(solution)/shard_map/all_gather | solution.py:212
  40.9 8.3 %collective-permute-start = (bf16[256,512]{1,0:T(8,128)(2,1)}, bf16[256,512]{1,0:T(8,128)(2,1)S(1)}, u32[]{:S(2)}, u32[]{:S(2)}) collective-permute-start(bf16[256,512]{1,0:T(8,128)(2,1)} %get-tuple-element.931), channel_id=1, source_target_pairs={{0,1},{1,0},{2,3},{3,2},{4,5},{5,4},{6,7},{7,6},{8,9},{9,8},{10,11... | collective-permute-start | bytes 786440 | tf_op jit(solution)/shard_map/ppermute | solution.py:14
  51.2 18.7 %collective-permute-start.1 = (bf16[512,512]{1,0:T(8,128)(2,1)}, bf16[512,512]{1,0:T(8,128)(2,1)}, u32[]{:S(2)}, u32[]{:S(2)}) collective-permute-start(bf16[512,512]{1,0:T(8,128)(2,1)} %maximum_select_fusion.1), channel_id=1, source_target_pairs={{0,2},{1,3},{2,0},{3,1},{4,6},{5,7},{6,4},{7,5},{8,10},{9,11},{10,... | collective-permute-start | bytes 1572872 | tf_op jit(solution)/shard_map/ppermute | solution.py:14
  56.9 102.4 %all-gather.9.cloned.1.call-start = ((), (), s32[]{:S(2)}) async-start(), calls=%async_computation.3 | async-start | bytes 1310720 | tf_op jit(solution)/shard_map/all_gather | solution.py:213
  103.5 0.8 copy-start.4
  104.4 271.3 %all-reduce.3.cloned.1.call-start = ((), (), s32[]{:S(2)}) async-start(), calls=%async_computation.5 | async-start | bytes 10485760 | tf_op jit(solution)/shard_map/psum | solution.py:223
  154.9 4.4 %copy-start.1 = (f32[256,512]{0,1:T(8,128)S(1)}, f32[256,512]{0,1:T(8,128)}, u32[]{:S(2)}) copy-start(f32[256,512]{0,1:T(8,128)} %custom-call.1) | copy-start | bytes 1572868
  169.1 3.3 copy-start.2
  173.9 0.8 copy-start.3
  184.5 3.3 copy-start.2
  189.3 0.8 copy-start.3
  199.9 3.3 copy-start.2
  204.8 0.8 copy-start.3
  215.3 3.3 copy-start.2
  220.2 0.8 copy-start.3
  232.0 1.0 copy-start.7
  375.7 5.0 %copy-start.9 = (f32[512,512]{1,0:T(8,128)S(1)}, f32[512,512]{1,0:T(8,128)}, u32[]{:S(2)}) copy-start(f32[512,512]{1,0:T(8,128)} %get-tuple-element.920) | copy-start | bytes 3145732
Sparse Core Ops, SparseCore 0:
  40.3 29.4 all-gather.4
  72.2 25.1 all-gather.10
  99.2 26.5 all-gather.6
  127.5 26.4 all-gather.8
  230.0 145.6 all-reduce.2
